TPU v7x, 256 devices: a whole 4x4x8 slice. The times are simulated.
256 devices in a mesh: sec: 32 (over z_hi, y, core), narrow: 8 (over x, z_lo).
Axes of the slice: x: 4, y: 4, z: 8 (z_hi: 4, z_lo: 2; z = z_hi * 2 + z_lo), core: 2. Of those that a mesh axis runs over, the one named last changes fastest.
Arguments:
- tokens: bfloat16 [4096, 2048], P('sec'), may hold values from -8 to 8
- attn_gain: float32 [2048], replicated, may hold values from 0.5 to 1.5
- w_query: bfloat16 [2048, 4096], P(None, 'narrow'), may hold values from -0.125 to 0.125
- w_key: bfloat16 [2048, 512], P(None, 'narrow'), may hold values from -0.125 to 0.125
- w_value: bfloat16 [2048, 512], P(None, 'narrow'), may hold values from -0.125 to 0.125
- query_gain: float32 [128], replicated, may hold values from 0.6 to 6
- key_gain: float32 [128], replicated, may hold values from 0.6 to 6
- w_out: bfloat16 [4096, 2048], P('narrow'), may hold values from -0.09375 to 0.09375
- moe_gain: float32 [2048], replicated, may hold values from 0.5 to 1.5
- expert_ids: int32 [4096, 8], P('sec'), may hold values from 0 to 127, all different within a row; in each aligned block of 16 rows (0 to 15, 16 to 31, ...) at most 2 rows name the same one
- expert_weights: float32 [4096, 8], P('sec'), may hold values from 0.05 to 1
- w_gate: bfloat16 [128, 2048, 768], P('sec', None, 'narrow'), may hold values from -0.125 to 0.125
- w_up: bfloat16 [128, 2048, 768], P('sec', None, 'narrow'), may hold values from -0.125 to 0.125
- w_down: bfloat16 [128, 768, 2048], P('sec', 'narrow'), may hold values from -0.21875 to 0.21875
Outputs:
- layer_out: bfloat16 [4096, 2048], P(('sec', 'narrow'))
Inputs may be any that keep to these rules, and one draw needn't show every extreme that they name: `expert_ids`: each row names 8 different experts. In each aligned block of 16 rows no expert is named by more than 2 rows, a bound that some block reaches.
All inputs are finite; a program needn't handle non-finite values.
Results may differ from a plain program's by a relative error of at most 0.009.
Values may be sent and summed in bfloat16 or wider, within the bound.
No kernel may reach another device: no remote copies, remote signals or barrier semaphores. Data moves between devices by JAX's collectives and lax.ppermute only.
A program may use at most 128 MiB of HBM per device.

v0:
```python
import math
import jax
import jax.numpy as jnp
from jax import lax
from jax.sharding import Mesh
from jax.sharding import PartitionSpec as P

D = 2048
HEADS = 32
KV_HEADS = 4
HEAD = 128
TOPK = 8
NARROW = ("narrow_0", "narrow_1")
SEC_NARROW = ("sec", "narrow_0", "narrow_1")
norm_eps = 1e-06


def gather_turned(arrays, axis, dims):
    turned = [jnp.moveaxis(a, dim, 0) for a, dim in zip(arrays, dims)]
    both = jnp.concatenate([t.reshape(len(t), -1) for t in turned], axis=1)
    whole, at, finished = (lax.all_gather(both, axis, axis=0, tiled=True), 0, [])
    for t, dim in zip(turned, dims):
        slab = whole[:, at : at + t[0].size].reshape(-1, *t.shape[1:])
        finished.append(jnp.moveaxis(slab, 0, dim))
        at += t[0].size
    return tuple(finished)


def sent_together(arrays, axis, dim, along):
    ends, at = ([], 0)
    for a in arrays[:-1]:
        at += a.shape[along]
        ends.append(at)
    both = jnp.concatenate(arrays, axis=along)
    return tuple(jnp.split(lax.all_gather(both, axis, axis=dim, tiled=True), ends, axis=along))


def in_blocks(x, dim, peers):
    shape = x.shape
    blocks = x.reshape(*shape[:dim], peers, shape[dim] // peers, *shape[dim + 1 :])
    return jnp.moveaxis(blocks, dim, 0)


def sum_at_owner(x, axis, dim):
    peers = lax.axis_size(axis)
    blocks = lax.all_to_all(in_blocks(x, dim, peers), axis, 0, 0, tiled=True)
    return jnp.sum(blocks.astype(jnp.float32), axis=0)


def sum_by_axis(terms, axes):
    running = terms.astype(jnp.bfloat16)
    for axis in axes:
        running = lax.psum_scatter(running, axis, scatter_dimension=0, tiled=True)
    return running.astype(jnp.float32)


def rms_norm(inputs, gain):
    widened = inputs.astype(jnp.float32)
    return (
        widened * lax.rsqrt(jnp.mean(widened * widened, axis=-1, keepdims=True) + norm_eps) * gain
    )


def rotate(inputs, positions):
    half_size = inputs.shape[-1] // 2
    inverse = jnp.exp(
        -jnp.log(1000000.0) * jnp.arange(half_size, dtype=jnp.float32) * 2.0 / inputs.shape[-1]
    )
    angles = positions.astype(jnp.float32)[:, None] * inverse[None, :]
    cosine = jnp.cos(angles)[:, None, :]
    sine = jnp.sin(angles)[:, None, :]
    leading = inputs[..., :half_size]
    trailing = inputs[..., half_size:]
    return jnp.concatenate(
        [leading * cosine - trailing * sine, trailing * cosine + leading * sine], axis=-1
    )


def slot_numbers(flat_ids, experts_all):
    onehot = (
        flat_ids[:, :, None] == jnp.arange(experts_all, dtype=jnp.int32)[None, None, :]
    ).astype(jnp.int32)
    earlier = jnp.cumsum(onehot, axis=1) - onehot
    return jnp.sum(earlier * onehot, axis=-1)


def head_columns(whole, kv_start, kv_here):
    width = whole.shape[0]
    strided = whole.reshape(width, HEAD, KV_HEADS)
    picked = lax.dynamic_slice_in_dim(strided, kv_start, kv_here, 2)
    return jnp.transpose(picked, (0, 2, 1)).reshape(width, kv_here * HEAD)


def on_device(
    tokens,
    attn_gain,
    w_query,
    w_key,
    w_value,
    query_gain,
    key_gain,
    w_out,
    moe_gain,
    expert_ids,
    expert_weights,
    w_gate,
    w_up,
    w_down,
):
    sec_count = lax.axis_size("sec")
    narrow_count = lax.axis_size(NARROW)
    sec_index = lax.axis_index("sec")
    narrow_index = lax.axis_index(NARROW)
    local_rows = tokens.shape[0]
    share_rows = local_rows // narrow_count
    expert_here = w_gate.shape[0]
    experts_all = expert_here * sec_count
    capacity = min(share_rows, max(2, 5 * share_rows * TOPK // (2 * experts_all)))
    heads_here = w_query.shape[1] // HEAD
    group_size = HEADS // KV_HEADS
    kv_here = max(1, heads_here // group_size)
    per_key_head = heads_here // kv_here
    kv_start = narrow_index * heads_here // group_size
    scale = 1.0 / math.sqrt(HEAD)
    positions = sec_index * local_rows + jnp.arange(local_rows, dtype=jnp.int32)
    last_position = sec_index * local_rows + local_rows - 1
    normed = rms_norm(tokens, attn_gain).astype(jnp.bfloat16)
    query = jnp.dot(normed, w_query, preferred_element_type=jnp.float32).reshape(
        local_rows, heads_here, HEAD
    )
    query = rotate(rms_norm(query, query_gain), positions).astype(jnp.bfloat16)
    key_whole, value_whole = gather_turned((w_key, w_value), NARROW, (1, 1))
    key_columns = head_columns(key_whole, kv_start, kv_here)
    value_columns = head_columns(value_whole, kv_start, kv_here)
    keys = jnp.dot(normed, key_columns, preferred_element_type=jnp.float32).reshape(
        local_rows, kv_here, HEAD
    )
    keys = (
        rotate(rms_norm(keys, key_gain), positions)
        .astype(jnp.bfloat16)
        .reshape(local_rows, kv_here * HEAD)
    )
    values = jnp.dot(normed, value_columns, preferred_element_type=jnp.float32).astype(jnp.bfloat16)
    grouped = query.reshape(local_rows, kv_here, per_key_head, HEAD)

    def update(state, block_keys, block_values, block_start):
        peak, total, accum = state
        width = block_keys.shape[0]
        scores = (
            jnp.einsum("tcgd,jcd->cgtj", grouped, block_keys, preferred_element_type=jnp.float32)
            * scale
        )
        key_positions = block_start + jnp.arange(width, dtype=jnp.int32)
        allowed = key_positions[None, :] <= positions[:, None]
        scores = jnp.where(allowed, scores, -1e30)
        new_peak = jnp.maximum(peak, jnp.max(scores, axis=-1))
        probs = jnp.where(allowed, jnp.exp(scores - new_peak[..., None]), 0.0)
        factor = jnp.exp(peak - new_peak)
        total = total * factor + jnp.sum(probs, axis=-1)
        accum = accum * factor[..., None] + jnp.einsum(
            "cgtj,jcd->cgtd",
            probs.astype(jnp.bfloat16),
            block_values,
            preferred_element_type=jnp.float32,
        )
        return (new_peak, total, accum)

    start_state = (
        jnp.full((kv_here, per_key_head, local_rows), -1e30, jnp.float32),
        jnp.zeros((kv_here, per_key_head, local_rows), jnp.float32),
        jnp.zeros((kv_here, per_key_head, local_rows, HEAD), jnp.float32),
    )
    carry = start_state
    key_piece, value_piece = sent_together((keys, values), "sec", 0, 1)
    length = key_piece.shape[0]
    width = math.gcd(length, 512)
    blocks = length // width
    key_blocks = key_piece.reshape(blocks, width, kv_here, HEAD)
    value_blocks = value_piece.reshape(blocks, width, kv_here, HEAD)

    def advance(state, inputs):
        block_keys, block_values, number = inputs
        block_start = number * width
        state = lax.cond(
            block_start <= last_position,
            lambda inner: update(inner, block_keys, block_values, block_start),
            lambda inner: inner,
            state,
        )
        return (state, None)

    carry, _ = lax.scan(
        advance, carry, (key_blocks, value_blocks, jnp.arange(blocks, dtype=jnp.int32))
    )
    peak, total, accum = carry
    attended = (
        jnp.transpose(accum / total[..., None], (2, 0, 1, 3))
        .reshape(local_rows, heads_here * HEAD)
        .astype(jnp.bfloat16)
    )
    own_offset = narrow_index * share_rows
    mixed = sum_at_owner(
        jnp.dot(attended, w_out, preferred_element_type=jnp.float32).astype(jnp.bfloat16), NARROW, 0
    )
    own_tokens = lax.dynamic_slice_in_dim(tokens, own_offset, share_rows, 0)
    carried_mine = (own_tokens.astype(jnp.float32) + mixed).astype(jnp.bfloat16)
    send_ids = lax.dynamic_slice_in_dim(expert_ids, own_offset, share_rows, 0)
    send_rows = rms_norm(carried_mine, moe_gain).astype(jnp.bfloat16)
    blocks_sent = 1

    def place(flat_ids, slots):
        return (flat_ids % expert_here * sec_count + flat_ids // expert_here) * capacity + slots

    out_rows = expert_here * sec_count * capacity
    flat_ids = send_ids.reshape(blocks_sent, share_rows * TOPK)
    slots = slot_numbers(flat_ids, experts_all)
    block_index = jnp.arange(blocks_sent, dtype=jnp.int32)[:, None]
    targets = block_index * out_rows + place(flat_ids, slots)
    sources = (
        block_index * share_rows + jnp.arange(share_rows * TOPK, dtype=jnp.int32)[None, :] // TOPK
    )
    table = (
        jnp.full((blocks_sent * out_rows,), blocks_sent * share_rows, jnp.int32)
        .at[targets.reshape(-1)]
        .set(sources.reshape(-1))
    )
    padded = jnp.concatenate([send_rows, jnp.zeros((1, D), jnp.bfloat16)], axis=0)
    outgoing = padded[table].reshape(blocks_sent, expert_here, sec_count, capacity, D)
    arrived = lax.all_to_all(outgoing, "sec", split_axis=2, concat_axis=2, tiled=True)
    piece = lax.all_gather(arrived, NARROW, axis=0, tiled=True)
    count = piece.shape[0]
    rows_in = piece.reshape(count, expert_here, sec_count * capacity, D)
    gate_value = jnp.einsum("berd,edf->berf", rows_in, w_gate, preferred_element_type=jnp.float32)
    up_value = jnp.einsum("berd,edf->berf", rows_in, w_up, preferred_element_type=jnp.float32)
    active = (jax.nn.silu(gate_value) * up_value).astype(jnp.bfloat16)
    number = out_rows * lax.axis_size(NARROW) // out_rows
    expert_total = sum_by_axis(
        jnp.einsum("berf,efd->berd", active, w_down, preferred_element_type=jnp.float32).reshape(
            out_rows * lax.axis_size(NARROW), D
        ),
        NARROW,
    ).astype(jnp.bfloat16)
    returned = lax.all_to_all(
        expert_total.reshape(1, expert_here, sec_count, capacity, D),
        "sec",
        split_axis=2,
        concat_axis=2,
        tiled=True,
    ).reshape(out_rows, D)
    own_ids = lax.dynamic_slice_in_dim(expert_ids, own_offset, share_rows, 0).reshape(
        1, share_rows * TOPK
    )
    own_slots = slot_numbers(own_ids, experts_all)
    picks = place(own_ids, own_slots).reshape(-1)
    gathered = returned[picks].reshape(share_rows, TOPK, D)
    own_weights = lax.dynamic_slice_in_dim(expert_weights, own_offset, share_rows, 0)
    gates = own_weights / jnp.sum(own_weights, axis=-1, keepdims=True)
    mixture = jnp.sum(gates[:, :, None] * gathered.astype(jnp.float32), axis=1)
    return (carried_mine.astype(jnp.float32) + mixture).astype(jnp.bfloat16)


def solution(mesh):
    split = Mesh(mesh.devices.reshape(mesh.shape["sec"], 4, 2), ("sec", "narrow_0", "narrow_1"))
    in_specs = (
        P("sec", None),
        P(),
        P(None, NARROW),
        P(None, NARROW),
        P(None, NARROW),
        P(),
        P(),
        P(NARROW, None),
        P(),
        P("sec", None),
        P("sec", None),
        P("sec", None, NARROW),
        P("sec", None, NARROW),
        P("sec", NARROW, None),
    )
    out_specs = P(SEC_NARROW, None)
    return jax.shard_map(
        on_device, mesh=split, in_specs=in_specs, out_specs=out_specs, check_vma=False
    )
```

profile of v0, /device:TPU:32, one launch (start us, length us, event | category | flops | bytes accessed | tf_op | source)
XLA Modules:
  0.0 678.0 jit_solution(6871199354798693213)
XLA Ops:
  9.9 94.0 %all-gather.4.cloned.1.call-done = bf16[512,4096]{1,0:T(8,128)(2,1)} async-done(((bf16[64,4096]{1,0:T(8,128)(2,1)}), bf16[512,4096]{1,0:T(8,128)(2,1)}) %all-gather.4.cloned.1.call-update) | async-done | bytes 4194320 | tf_op jit(solution)/shard_map/all_gather | solution.py:21
  103.9 4.8 slice_bitcast_fusion.1
  108.7 4.1 reshape.600
  112.8 4.1 reshape.601
  116.9 5.4 constant_dynamic-slice_fusion.1
  122.3 3.5 copy.62
  135.7 51.2 %all-gather.6.cloned.1.call-done = bf16[4096,256]{0,1:T(8,128)(2,1)} async-done(((bf16[128,256]{0,1:T(8,128)(2,1)}), bf16[4096,256]{0,1:T(8,128)(2,1)}) %all-gather.6.cloned.1.call-update) | async-done | bytes 2097168 | tf_op jit(solution)/shard_map/all_gather | solution.py:35
  186.9 2.7 fusion.73
  189.6 2.3 copy.81
  193.3 13.3 %while.15 = (s32[]{:T(128)}, f32[1,4,128]{2,1,0:T(4,128)S(1)}, f32[1,4,128]{2,1,0:T(4,128)S(1)}, f32[1,4,128,128]{3,2,1,0:T(8,128)S(1)}, s32[8]{0:T(128)S(1)}, /...) while((s32[]{:T(128)}, f32[1,4,128]{2,1,0:T(4,128)S(1)}, ...), condition=%wide.region_8.9_spmd.clone, body=%wide.region_3.8_spmd.clone.sunk | while | flops 136775808 | bytes 4365611 | solution.py:192
  194.5 3.0 conditional.3
  208.1 6.7 all-to-all-start
  216.3 7.8 %all-to-all-done = bf16[8,16,2048]{2,1,0:T(8,128)(2,1)S(1)} async-done(((bf16[8,16,2048]{2,1,0:T(8,128)(2,1)}), bf16[8,16,2048]{2,1,0:T(8,128)(2,1)S(1)}, u32[]{:S(2)}, u32[]{:S(2)}) %all-to-all-start) | async-done | bytes 524320 | tf_op jit(solution)/shard_map/all_to_all | solution.py:46
  228.5 52.3 %all_to_all.15 = bf16[1,4,32,2,2048]{4,3,0,1,2:T(2,128)(2,1)} all-to-all(bf16[1,4,32,2,2048]{4,3,0,1,2:T(2,128)(2,1)S(1)} %copy.72), channel_id=1, replica_groups=mesh['sec'=32,'narrow_0'=4,'narrow_1'=2] {'sec'}, dimensions={2} | all-to-all | bytes 2097152 | tf_op jit(solution)/shard_map/all_to_all | solution.py:229
  281.0 169.5 %all-gather.8.cloned.1.call-done = bf16[8,4,32,2,2048]{4,3,0,1,2:T(2,128)(2,1)} async-done(((bf16[1,4,32,2,2048]{4,3,0,1,2:T(2,128)(2,1)}), bf16[8,4,32,2,2048]{4,3,0,1,2:T(2,128)(2,1)}) %all-gather.8.cloned.1.call-update) | async-done | bytes 8388624 | tf_op jit(solution)/shard_map/all_gather | solution.py:230
  450.5 8.2 %copy.73 = bf16[8,4,32,2,2048]{4,3,2,0,1:T(2,128)(2,1)} copy(bf16[8,4,32,2,2048]{4,3,0,1,2:T(2,128)(2,1)} %all-gather.8.cloned.1.call-done) | data formatting | bytes 16777216 | tf_op jit(solution)/shard_map/all_gather | solution.py:230
  458.7 13.1 %reshape.608 = bf16[8,4,64,2048]{3,2,0,1:T(8,128)(2,1)} reshape(bf16[8,4,32,2,2048]{4,3,2,0,1:T(2,128)(2,1)} %copy.73) | data formatting | bytes 16777216 | tf_op jit(solution)/shard_map/reshape | solution.py:232
  471.8 6.1 fusion.26
  477.9 12.0 %convert_bitcast_fusion = bf16[8,4,64,2048]{3,2,0,1:T(8,128)(2,1)} fusion(bf16[4,96,2048]{2,1,0:T(8,128)(2,1)} %param.31, bf16[8,4,64,2048]{3,2,0,1:T(8,128)(2,1)} %reshape.608, bf16[4,2048,96]{1,2,0:T(8,128)(2,1)} %param.30, f32[8,4,64,96]{3,2,0,1:T(8,128)S(1)} %fusion.26), kind=kOutput, calls=%fused_computation.31 | convolution fusion | flops 1615986688 | bytes 20709376 | tf_op jit(solution)/shard_map/berf,efd->berd/dot_general | solution.py:238
  489.9 8.3 %copy.74 = bf16[8,4,64,2048]{3,2,1,0:T(8,128)(2,1)} copy(bf16[8,4,64,2048]{3,2,0,1:T(8,128)(2,1)} %convert_bitcast_fusion) | data formatting | bytes 16777216 | tf_op jit(solution)/shard_map/convert_element_type | solution.py:51
  498.2 84.2 %reduce-scatter.3.cloned.1.call-done = bf16[512,2048]{1,0:T(8,128)(2,1)} async-done(((bf16[2048,2048]{1,0:T(8,128)(2,1)}), bf16[512,2048]{1,0:T(8,128)(2,1)}) %reduce-scatter.3.cloned.1.call-update) | async-done | bytes 2097168 | tf_op jit(solution)/shard_map/reduce_scatter | solution.py:53
  582.5 37.9 %reduce-scatter.5.cloned.1.call-done = bf16[256,2048]{1,0:T(8,128)(2,1)} async-done(((bf16[512,2048]{1,0:T(8,128)(2,1)}), bf16[256,2048]{1,0:T(8,128)(2,1)}) %reduce-scatter.5.cloned.1.call-update) | async-done | bytes 1048592 | tf_op jit(solution)/shard_map/reduce_scatter | solution.py:53
  624.3 10.1 %all-to-all-start.2 = ((bf16[1,4,32,2,2048]{4,3,1,0,2:T(2,128)(2,1)}), bf16[1,4,32,2,2048]{4,3,1,0,2:T(2,128)(2,1)S(1)}, u32[]{:S(2)}, u32[]{:S(2)}) async-start(bf16[1,4,32,2,2048]{4,3,1,0,2:T(2,128)(2,1)} %copy.75), calls=%async_computation.4 | async-start | bytes 2097152 | tf_op jit(solution)/shard_map/all_to_all | solution.py:243
  634.6 29.6 %all-to-all-done.2 = bf16[1,4,32,2,2048]{4,3,1,0,2:T(2,128)(2,1)S(1)} async-done(((bf16[1,4,32,2,2048]{4,3,1,0,2:T(2,128)(2,1)}), bf16[1,4,32,2,2048]{4,3,1,0,2:T(2,128)(2,1)S(1)}, u32[]{:S(2)}, u32[]{:S(2)}) %all-to-all-start.2) | async-done | bytes 1048608 | tf_op jit(solution)/shard_map/all_to_all | solution.py:243
  (118 shorter events, 41.1 us)
Async XLA Ops:
  6.5 200.3 %copy-start = (bf16[512,2048]{1,0:T(8,128)(2,1)S(1)}, bf16[512,2048]{1,0:T(8,128)(2,1)}, u32[]{:S(2)}) copy-start(bf16[512,2048]{1,0:T(8,128)(2,1)} %param.25) | copy-start | bytes 6291460
  6.5 97.3 %all-gather.4.cloned.1.call-start = ((), (), s32[]{:S(2)}) async-start(), calls=%async_computation.5 | async-start | bytes 4718592 | tf_op jit(solution)/shard_map/all_gather | solution.py:21
  8.6 178.3 %all-gather.6.cloned.1.call-start = ((), (), s32[]{:S(2)}) async-start(), calls=%async_computation.6 | async-start | bytes 2162688 | tf_op jit(solution)/shard_map/all_gather | solution.py:35
  116.9 8.9 %copy-start.3 = (f32[2048]{0:T(1024)S(1)}, f32[2048]{0:T(1024)}, u32[]{:S(2)}) copy-start(f32[2048]{0:T(1024)} %param.19) | copy-start | bytes 24580
  125.8 5.1 copy-start.6
  125.8 6.1 copy-start.5
  131.3 4.0 copy-start.7
  206.8 18.4 %copy-start.4 = (f32[2048]{0:T(1024)S(1)}, f32[2048]{0:T(1024)}, u32[]{:S(2)}) copy-start(f32[2048]{0:T(1024)} %param.26) | copy-start | bytes 24580
  208.1 16.1 %all-to-all-start = ((bf16[8,16,2048]{2,1,0:T(8,128)(2,1)}), bf16[8,16,2048]{2,1,0:T(8,128)(2,1)S(1)}, u32[]{:S(2)}, u32[]{:S(2)}) async-start(bf16[8,16,2048]{2,1,0:T(8,128)(2,1)} %bitcast.29), calls=%async_computation | async-start | bytes 1048576 | tf_op jit(solution)/shard_map/all_to_all | solution.py:46
  214.8 235.7 %all-gather.8.cloned.1.call-start = ((), (), s32[]{:S(2)}) async-start(), calls=%async_computation.7 | async-start | bytes 9437184 | tf_op jit(solution)/shard_map/all_gather | solution.py:230
  280.8 301.7 %reduce-scatter.3.cloned.1.call-start = ((), (), s32[]{:S(2)}) async-start(), calls=%async_computation.8 | async-start | bytes 10485760 | tf_op jit(solution)/shard_map/reduce_scatter | solution.py:53
  498.2 122.2 %reduce-scatter.5.cloned.1.call-start = ((), (), s32[]{:S(2)}) async-start(), calls=%async_computation.9 | async-start | bytes 3145728 | tf_op jit(solution)/shard_map/reduce_scatter | solution.py:53
  622.1 12.2 %copy-start.2 = (f32[128,8]{0,1:T(8,128)S(1)}, f32[128,8]{0,1:T(8,128)}, u32[]{:S(2)}) copy-start(f32[128,8]{0,1:T(8,128)} %param.28) | copy-start | bytes 12292
  624.3 39.9 %all-to-all-start.2 = ((bf16[1,4,32,2,2048]{4,3,1,0,2:T(2,128)(2,1)}), bf16[1,4,32,2,2048]{4,3,1,0,2:T(2,128)(2,1)S(1)}, u32[]{:S(2)}, u32[]{:S(2)}) async-start(bf16[1,4,32,2,2048]{4,3,1,0,2:T(2,128)(2,1)} %copy.75), calls=%async_computation.4 | async-start | bytes 2097152 | tf_op jit(solution)/shard_map/all_to_all | solution.py:243
  666.0 5.5 copy-start.1
Sparse Core Ops, SparseCore 0:
  9.1 94.7 all-gather.3
  132.0 54.8 all-gather.5
  280.9 169.5 all-gather.7
  498.3 84.1 reduce-scatter.2
  584.8 35.5 reduce-scatter.4
where the time goes:
time: 680 us; the launch traced here: 678 us
  waiting for transfers between devices  474 us (70%)
  local copies, waits for them, and re-layouts  78.3 us (12%)
  blocking collectives  52.3 us (8%)
  matrix products  27.4 us (4%)
  starting transfers between devices  17.1 us (3%)
  between operations  13.5 us (2%)
  other arithmetic  9.42 us (1%)
    all_gather x1, waiting for transfers between devices, on_device(): piece = lax.all_gather(arrived, NARROW, axis=0, tiled=True)  169 us
    reduce_scatter x2, waiting for transfers between devices, sum_by_axis(): running = lax.psum_scatter(running, axis, scatter_dimension=0, tiled=True)  122 us
    all_gather x1, waiting for transfers between devices, gather_turned(): lax.all_gather(both, axis, axis=0, tiled=True)  94 us
    all_to_all x1, blocking collectives, on_device(): lax.all_to_all(outgoing, 'sec', split_axis=2, concat_axis=2, tiled=True)  52.3 us
    all_gather x1, waiting for transfers between devices, sent_together(): lax.all_gather(both, axis, axis=dim, tiled=True)  51.2 us
    all_to_all x1, waiting for transfers between devices, on_device(): lax.all_to_all(expert_total.reshape(1, expert_here, sec_count, capacity,...  29.6 us
  transfers between devices with their start and end apart: 7, of which 7 were waited for; matrix products, arithmetic and copies ran while one was open for 1% of the time, Pallas kernels for 0%

commit v1 on v0

--- a/solution.py
+++ b/solution.py
@@ -227,7 +227,9 @@
     padded = jnp.concatenate([send_rows, jnp.zeros((1, D), jnp.bfloat16)], axis=0)
     outgoing = padded[table].reshape(blocks_sent, expert_here, sec_count, capacity, D)
     arrived = lax.all_to_all(outgoing, "sec", split_axis=2, concat_axis=2, tiled=True)
-    piece = lax.all_gather(arrived, NARROW, axis=0, tiled=True)
+    piece = jnp.concatenate(
+        lax.all_to_all(jnp.stack([arrived] * lax.axis_size(NARROW)), NARROW, 0, 0), axis=0
+    )
     count = piece.shape[0]
     rows_in = piece.reshape(count, expert_here, sec_count * capacity, D)
     gate_value = jnp.einsum("berd,edf->berf", rows_in, w_gate, preferred_element_type=jnp.float32)

time: 680 us -> 605 us (0.89)
  waiting for transfers between devices: 474 us -> 299 us
  blocking collectives: 52.3 us -> 155 us
    all_gather x1 -> x0, waiting for transfers between devices: 169 us -> none  [on_device(): piece = lax.all_gather(arrived, NARROW, axis=0, tiled=True)]
    all_to_all x0 -> x1, blocking collectives: none -> 103 us  [on_device(): lax.all_to_all(jnp.stack([arrived] * lax.axis_size(NARROW)), NARROW, 0, 0)]
    another operation x0 -> x2, local copies, waits for them, and re-layouts: none -> 18.9 us  [the longest x1 13.2 us: on_device(): rows_in = piece.reshape(count, expert_here, sec_count * capacity, D)]
    reshape x1 -> x0, local copies, waits for them, and re-layouts: 13.1 us -> none  [on_device(): rows_in = piece.reshape(count, expert_here, sec_count * capacity, D)]
    all_gather x1 -> x0, local copies, waits for them, and re-layouts: 8.16 us -> none  [on_device(): piece = lax.all_gather(arrived, NARROW, axis=0, tiled=True)]
  transfers between devices with their start and end apart: 7 -> 6, of which waited for: 7 -> 6; matrix products, arithmetic and copies ran while one was open for 1% -> 1% of each run, Pallas kernels for 0% -> 0%
where the time goes in v1:
time: 605 us; the launch traced here: 603 us
  waiting for transfers between devices  299 us (49%)
  blocking collectives  155 us (26%)
  local copies, waits for them, and re-layouts  76.8 us (13%)
  matrix products  27 us (4%)
  starting transfers between devices  16.9 us (3%)
  between operations  13.5 us (2%)
  other arithmetic  9.43 us (2%)
    reduce_scatter x2, waiting for transfers between devices, sum_by_axis(): running = lax.psum_scatter(running, axis, scatter_dimension=0, tiled=True)  116 us
    all_to_all x1, blocking collectives, on_device(): lax.all_to_all(jnp.stack([arrived] * lax.axis_size(NARROW)), NARROW, 0, 0)  103 us
    all_gather x1, waiting for transfers between devices, gather_turned(): lax.all_gather(both, axis, axis=0, tiled=True)  94 us
    all_to_all x1, blocking collectives, on_device(): lax.all_to_all(outgoing, 'sec', split_axis=2, concat_axis=2, tiled=True)  52.1 us
    all_gather x1, waiting for transfers between devices, sent_together(): lax.all_gather(both, axis, axis=dim, tiled=True)  51.2 us
    all_to_all x1, waiting for transfers between devices, on_device(): lax.all_to_all(expert_total.reshape(1, expert_here, sec_count, capacity,...  29.6 us
    another operation x1, local copies, waits for them, and re-layouts, on_device(): rows_in = piece.reshape(count, expert_here, sec_count * capacity, D)  13.2 us
  transfers between devices with their start and end apart: 6, of which 6 were waited for; matrix products, arithmetic and copies ran while one was open for 1% of the time, Pallas kernels for 0%

profile of v1, /device:TPU:32, one launch (start us, length us, event | category | flops | bytes accessed | tf_op | source)
XLA Modules:
  0.0 603.2 jit_solution(1720929058779982423)
XLA Ops:
  9.9 94.0 %all-gather.3.cloned.1.call-done = bf16[512,4096]{1,0:T(8,128)(2,1)} async-done(((bf16[64,4096]{1,0:T(8,128)(2,1)}), bf16[512,4096]{1,0:T(8,128)(2,1)}) %all-gather.3.cloned.1.call-update) | async-done | bytes 4194320 | tf_op jit(solution)/shard_map/all_gather | solution.py:21
  103.9 4.8 slice_bitcast_fusion.1
  108.7 4.1 reshape.600
  112.8 4.1 reshape.601
  116.9 5.4 constant_dynamic-slice_fusion.1
  122.3 3.5 copy.60
  135.7 51.2 %all-gather.5.cloned.1.call-done = bf16[4096,256]{0,1:T(8,128)(2,1)} async-done(((bf16[128,256]{0,1:T(8,128)(2,1)}), bf16[4096,256]{0,1:T(8,128)(2,1)}) %all-gather.5.cloned.1.call-update) | async-done | bytes 2097168 | tf_op jit(solution)/shard_map/all_gather | solution.py:35
  186.9 2.7 fusion.88
  189.6 2.3 copy.80
  193.3 13.4 %while.15 = (s32[]{:T(128)}, f32[1,4,128]{2,1,0:T(4,128)S(1)}, f32[1,4,128]{2,1,0:T(4,128)S(1)}, f32[1,4,128,128]{3,2,1,0:T(8,128)S(1)}, s32[8]{0:T(128)S(1)}, /...) while((s32[]{:T(128)}, f32[1,4,128]{2,1,0:T(4,128)S(1)}, ...), condition=%wide.region_8.9_spmd.clone, body=%wide.region_3.8_spmd.clone.sunk | while | flops 136775808 | bytes 4365611 | solution.py:192
  194.5 3.0 conditional.3
  208.1 6.7 %all-to-all-start = ((bf16[8,16,2048]{2,1,0:T(8,128)(2,1)}), bf16[8,16,2048]{2,1,0:T(8,128)(2,1)S(1)}, u32[]{:S(2)}, u32[]{:S(2)}) async-start(bf16[8,16,2048]{2,1,0:T(8,128)(2,1)} %bitcast.29), calls=%async_computation | async-start | bytes 1048576 | tf_op jit(solution)/shard_map/all_to_all | solution.py:46
  216.3 7.8 %all-to-all-done = bf16[8,16,2048]{2,1,0:T(8,128)(2,1)S(1)} async-done(((bf16[8,16,2048]{2,1,0:T(8,128)(2,1)}), bf16[8,16,2048]{2,1,0:T(8,128)(2,1)S(1)}, u32[]{:S(2)}, u32[]{:S(2)}) %all-to-all-start) | async-done | bytes 524320 | tf_op jit(solution)/shard_map/all_to_all | solution.py:46
  228.5 52.1 %all_to_all.23 = bf16[1,4,32,2,2048]{4,3,1,0,2:T(2,128)(2,1)S(1)} all-to-all(bf16[1,4,32,2,2048]{4,3,1,0,2:T(2,128)(2,1)S(1)} %copy.70), channel_id=1, replica_groups=mesh['sec'=32,'narrow_0'=4,'narrow_1'=2] {'sec'}, dimensions={2} | all-to-all | bytes 2097152 | tf_op jit(solution)/shard_map/all_to_all | solution.py:229
  281.4 5.7 stack.2
  287.1 102.8 %all_to_all.24 = bf16[8,1,4,32,2,2048]{5,4,3,2,1,0:T(2,128)(2,1)} all-to-all(bf16[8,1,4,32,2,2048]{5,4,3,2,1,0:T(2,128)(2,1)S(1)} %stack.2), channel_id=1, replica_groups=mesh['sec'=32,'narrow_0'=4,'narrow_1'=2] {'narrow_0','narrow_1'}, dimensions={0} | all-to-all | bytes 16777216 | tf_op jit(solution)/shard_map/all_to_all | solution.py:231
  389.9 13.2 %reshape.641 = bf16[8,4,64,2048]{3,2,1,0:T(8,128)(2,1)} reshape(bf16[8,1,4,32,2,2048]{5,4,3,2,1,0:T(2,128)(2,1)} %all_to_all.24) | data formatting | bytes 16777216 | tf_op jit(solution)/shard_map/reshape;reshape | solution.py:234
  403.1 5.7 fusion.28
  408.8 12.0 %convert_bitcast_fusion = bf16[8,4,64,2048]{3,2,0,1:T(8,128)(2,1)} fusion(bf16[4,96,2048]{2,1,0:T(8,128)(2,1)} %param.31, bf16[4,2048,96]{1,2,0:T(8,128)(2,1)} %param.30, bf16[8,4,64,2048]{3,2,1,0:T(8,128)(2,1)} %reshape.641, f32[8,4,64,96]{3,2,0,1:T(8,128)S(1)} %fusion.28), kind=kOutput, calls=%fused_computation.31 | convolution fusion | flops 1615986688 | bytes 20709376 | tf_op jit(solution)/shard_map/berf,efd->berd/dot_general | solution.py:240
  420.8 8.3 %copy.73 = bf16[8,4,64,2048]{3,2,1,0:T(8,128)(2,1)} copy(bf16[8,4,64,2048]{3,2,0,1:T(8,128)(2,1)} %convert_bitcast_fusion) | data formatting | bytes 16777216 | tf_op jit(solution)/shard_map/convert_element_type | solution.py:51
  429.2 78.5 %reduce-scatter.3.cloned.1.call-done = bf16[512,2048]{1,0:T(8,128)(2,1)} async-done(((bf16[2048,2048]{1,0:T(8,128)(2,1)}), bf16[512,2048]{1,0:T(8,128)(2,1)}) %reduce-scatter.3.cloned.1.call-update) | async-done | bytes 2097168 | tf_op jit(solution)/shard_map/reduce_scatter | solution.py:53
  507.7 37.9 %reduce-scatter.5.cloned.1.call-done = bf16[256,2048]{1,0:T(8,128)(2,1)} async-done(((bf16[512,2048]{1,0:T(8,128)(2,1)}), bf16[256,2048]{1,0:T(8,128)(2,1)}) %reduce-scatter.5.cloned.1.call-update) | async-done | bytes 1048592 | tf_op jit(solution)/shard_map/reduce_scatter | solution.py:53
  549.5 10.1 %all-to-all-start.3 = ((bf16[1,4,32,2,2048]{4,3,1,0,2:T(2,128)(2,1)}), bf16[1,4,32,2,2048]{4,3,1,0,2:T(2,128)(2,1)S(1)}, u32[]{:S(2)}, u32[]{:S(2)}) async-start(bf16[1,4,32,2,2048]{4,3,1,0,2:T(2,128)(2,1)} %copy.74), calls=%async_computation.5 | async-start | bytes 2097152 | tf_op jit(solution)/shard_map/all_to_all | solution.py:245
  559.8 29.6 %all-to-all-done.3 = bf16[1,4,32,2,2048]{4,3,1,0,2:T(2,128)(2,1)S(1)} async-done(((bf16[1,4,32,2,2048]{4,3,1,0,2:T(2,128)(2,1)}), bf16[1,4,32,2,2048]{4,3,1,0,2:T(2,128)(2,1)S(1)}, u32[]{:S(2)}, u32[]{:S(2)}) %all-to-all-start.3) | async-done | bytes 1048608 | tf_op jit(solution)/shard_map/all_to_all | solution.py:245
  (119 shorter events, 41.7 us)
Async XLA Ops:
  6.5 200.3 %copy-start = (bf16[512,2048]{1,0:T(8,128)(2,1)S(1)}, bf16[512,2048]{1,0:T(8,128)(2,1)}, u32[]{:S(2)}) copy-start(bf16[512,2048]{1,0:T(8,128)(2,1)} %param.25) | copy-start | bytes 6291460
  6.5 97.3 %all-gather.3.cloned.1.call-start = ((), (), s32[]{:S(2)}) async-start(), calls=%async_computation.6 | async-start | bytes 4718592 | tf_op jit(solution)/shard_map/all_gather | solution.py:21
  8.6 178.4 %all-gather.5.cloned.1.call-start = ((), (), s32[]{:S(2)}) async-start(), calls=%async_computation.7 | async-start | bytes 2162688 | tf_op jit(solution)/shard_map/all_gather | solution.py:35
  116.9 8.9 %copy-start.3 = (f32[2048]{0:T(1024)S(1)}, f32[2048]{0:T(1024)}, u32[]{:S(2)}) copy-start(f32[2048]{0:T(1024)} %param.19) | copy-start | bytes 24580
  125.8 5.1 copy-start.6
  125.8 6.1 %copy-start.5 = (s32[128,8]{0,1:T(8,128)S(1)}, s32[128,8]{0,1:T(8,128)}, u32[]{:S(2)}) copy-start(s32[128,8]{0,1:T(8,128)} %param.27) | copy-start | bytes 12292
  131.3 4.0 copy-start.7
  206.8 18.4 %copy-start.4 = (f32[2048]{0:T(1024)S(1)}, f32[2048]{0:T(1024)}, u32[]{:S(2)}) copy-start(f32[2048]{0:T(1024)} %param.26) | copy-start | bytes 24580
  208.1 16.0 %all-to-all-start = ((bf16[8,16,2048]{2,1,0:T(8,128)(2,1)}), bf16[8,16,2048]{2,1,0:T(8,128)(2,1)S(1)}, u32[]{:S(2)}, u32[]{:S(2)}) async-start(bf16[8,16,2048]{2,1,0:T(8,128)(2,1)} %bitcast.29), calls=%async_computation | async-start | bytes 1048576 | tf_op jit(solution)/shard_map/all_to_all | solution.py:46
  214.8 292.8 %reduce-scatter.3.cloned.1.call-start = ((), (), s32[]{:S(2)}) async-start(), calls=%async_computation.8 | async-start | bytes 10485760 | tf_op jit(solution)/shard_map/reduce_scatter | solution.py:53
  389.9 13.2 %copy-start.8 = (bf16[4,2048,96]{1,2,0:T(8,128)(2,1)S(1)}, bf16[4,2048,96]{1,2,0:T(8,128)(2,1)}, u32[]{:S(2)}) copy-start(bf16[4,2048,96]{1,2,0:T(8,128)(2,1)} %param.29) | copy-start | bytes 4718596
  429.1 116.5 %reduce-scatter.5.cloned.1.call-start = ((), (), s32[]{:S(2)}) async-start(), calls=%async_computation.9 | async-start | bytes 3145728 | tf_op jit(solution)/shard_map/reduce_scatter | solution.py:53
  547.3 12.2 %copy-start.2 = (f32[128,8]{0,1:T(8,128)S(1)}, f32[128,8]{0,1:T(8,128)}, u32[]{:S(2)}) copy-start(f32[128,8]{0,1:T(8,128)} %param.28) | copy-start | bytes 12292
  549.5 39.9 %all-to-all-start.3 = ((bf16[1,4,32,2,2048]{4,3,1,0,2:T(2,128)(2,1)}), bf16[1,4,32,2,2048]{4,3,1,0,2:T(2,128)(2,1)S(1)}, u32[]{:S(2)}, u32[]{:S(2)}) async-start(bf16[1,4,32,2,2048]{4,3,1,0,2:T(2,128)(2,1)} %copy.74), calls=%async_computation.5 | async-start | bytes 2097152 | tf_op jit(solution)/shard_map/all_to_all | solution.py:245
  591.2 5.5 copy-start.1
Sparse Core Ops, SparseCore 0:
  9.1 94.7 all-gather.2
  132.1 54.8 all-gather.4
  429.3 78.3 reduce-scatter.2
  510.0 35.5 reduce-scatter.4
